TPU v7x, 32 devices: a whole 2x2x4 slice. The times are simulated.
32 devices in a mesh: sector: 16 (over z, y, x), op: 2 (over core).
Axes of the slice: x: 2, y: 2, z: 4, core: 2. Of those that a mesh axis runs over, the one named last changes fastest.
Arguments:
- psi: bfloat16 [1024, 128, 128], P('sector'), may hold values from -6 to 6
- left_env: bfloat16 [2, 128, 128, 128], P('op', 'sector'), may hold values from -0.5 to 0.5
- right_env: bfloat16 [2, 128, 128, 128], P('op', 'sector'), may hold values from -0.375 to 0.375
- left_dims: int32 [128], replicated, may hold values from 64 to 128
- right_dims: int32 [128], replicated, may hold values from 64 to 128
- block_right: int32 [1024], replicated, may hold values from 0 to 127, as said below
Outputs:
- h_psi: bfloat16 [1024, 128, 128], P('sector', 'op')
Inputs may be any that keep to these rules, and one draw needn't show every extreme that they name: Block d * 64 + j lies in left sector d * 8 + j // 8; its right sector is owned by index block_right // 8 of sector, and block_right % 8 equals j // 8. Of the 64 blocks of each index of sector, exactly 4 have their right sector owned by each index of sector; the 8 blocks of one left sector have distinct right sectors, and every right sector is paired with exactly 8 blocks.
All inputs are finite; a program needn't handle non-finite values.
Results may differ from a plain program's by a relative error of at most 0.0049.
Values may be sent and summed in bfloat16 or wider, within the bound.
A program may use at most 64 MiB of HBM per device.

v0:
```python
import jax
import jax.numpy as jnp
from jax import lax
from jax.sharding import PartitionSpec as P


def combine(partial_sum):
    row_count = partial_sum.shape[1] // lax.axis_size("op")
    whole = lax.psum(partial_sum, "op")
    return lax.dynamic_slice_in_dim(whole, lax.axis_index("op") * row_count, row_count, 1)


def per_device(psi, left_env, right_env, left_dims, right_dims, block_right):
    devices = lax.axis_size("sector")
    sector_index = lax.axis_index("sector")
    blocks = psi.shape[0]
    block_width = psi.shape[1]
    term_count = left_env.shape[0]
    sectors = left_env.shape[1]
    coupled = blocks // sectors
    slot_count = blocks // devices
    counter = jnp.arange(blocks, dtype=jnp.int32)
    mine_right = lax.dynamic_slice_in_dim(block_right, sector_index * blocks, blocks)
    mine_owner = mine_right // sectors
    send_order = jnp.argsort(mine_owner * blocks + counter)
    inverse = jnp.argsort(send_order)
    own_dims = lax.dynamic_slice_in_dim(left_dims, sector_index * sectors, sectors)
    row_limit = jnp.repeat(own_dims, coupled)
    col_limit = right_dims[mine_right]
    position = jnp.arange(block_width, dtype=jnp.int32)
    keep_mask = (position[None, :, None] < row_limit[:, None, None]) & (
        position[None, None, :] < col_limit[:, None, None]
    )
    masked = psi * keep_mask.astype(psi.dtype)
    products = jnp.einsum(
        "ksab,snbc->ksnac",
        left_env,
        masked.reshape(sectors, coupled, block_width, block_width),
        preferred_element_type=jnp.float32,
    )
    products = products.astype(jnp.bfloat16).reshape(term_count, blocks, block_width, block_width)
    owners_all = (block_right // sectors).reshape(devices, blocks)
    foreign = (owners_all != sector_index).astype(jnp.int32)
    incoming = jnp.argsort(foreign * blocks + counter[None, :], axis=1)[:, :slot_count]
    arriving = (
        jnp.take_along_axis(block_right.reshape(devices, blocks), incoming, axis=1).reshape(-1)
        - sector_index * sectors
    )
    outgoing = right_env[:, arriving].reshape(
        term_count, devices, slot_count, block_width, block_width
    )
    received = lax.all_to_all(outgoing, "sector", split_axis=1, concat_axis=1, tiled=True)
    chosen = received.reshape(term_count, blocks, block_width, block_width)[:, inverse]
    partial_sum = jnp.einsum("kjab,kjcb->jac", products, chosen, preferred_element_type=jnp.float32)
    result = combine(partial_sum).astype(jnp.bfloat16)
    row_count = result.shape[1]
    op_index = lax.axis_index("op")
    row_position = op_index * row_count + jnp.arange(row_count, dtype=jnp.int32)
    keep_rows = (row_position[None, :, None] < row_limit[:, None, None]) & (
        position[None, None, :] < col_limit[:, None, None]
    )
    return result * keep_rows.astype(jnp.bfloat16)


def solution(mesh):
    in_specs = (
        P("sector", None, None),
        P("op", "sector", None, None),
        P("op", "sector", None, None),
        P(),
        P(),
        P(),
    )
    out_specs = P("sector", "op", None)
    return jax.shard_map(
        per_device, mesh=mesh, in_specs=in_specs, out_specs=out_specs, check_vma=False
    )
```

profile of v0, /device:TPU:13, one launch (start us, length us, event | category | flops | bytes accessed | tf_op | source)
XLA Modules:
  0.0 86.6 jit_solution(15736413275250530421)
XLA Ops:
  0.0 0.8 reshape.167
  0.8 0.7 fusion.4
  1.6 0.1 copy.23
  1.7 1.0 %sort.48 = (s32[16,64]{0,1:T(8,128)}, s32[16,64]{0,1:T(8,128)S(1)}) sort(s32[16,64]{0,1:T(8,128)S(1)} %iota_add_fusion, s32[16,64]{0,1:T(8,128)S(1)} %iota.41), dimensions={1}, to_apply=%region_0.1 | sort | flops 10240 | bytes 16384 | tf_op jit(solution)/shard_map/jit(argsort)/sort | solution.py:44
  2.7 0.1 copy.24
  2.8 0.1 reshape.200
  2.9 0.8 gather_fusion.3
  3.8 0.1 copy.25
  3.9 0.1 copy.26
  4.0 0.1 sub.31
  4.1 2.2 %gather_fusion.1 = bf16[64,128,128]{2,1,0:T(8,128)(2,1)} fusion(bf16[8,128,128]{2,1,0:T(8,128)(2,1)S(1)} %bitcast.24, s32[1024]{0:T(1024)S(1)} %pad_clamp_fusion.1), kind=kCustom, calls=%fused_computation.1 | custom fusion | bytes 4194560 | tf_op jit(solution)/shard_map/gather | solution.py:49
  6.3 6.7 %all-to-all-start = ((bf16[1,16,4,128,128]{4,3,2,0,1:T(8,128)(2,1)}), bf16[1,16,4,128,128]{4,3,2,0,1:T(8,128)(2,1)S(1)}, u32[]{:S(2)}, u32[]{:S(2)}) async-start(bf16[1,16,4,128,128]{4,3,2,0,1:T(8,128)(2,1)} %bitcast.26), calls=%async_computation | async-start | bytes 4194304 | tf_op jit(solution)/shard_map/all_to_all | solution.py:52
  13.2 0.8 iota_add_fusion.1
  14.0 0.8 gather_fusion
  14.8 2.0 %sort.49 = (s32[64]{0:T(128)}, s32[64]{0:T(128)S(1)}) sort(s32[64]{0:T(128)S(1)} %get-tuple-element.11, s32[64]{0:T(128)S(1)} %iota.43), dimensions={0}, to_apply=%region_1.2 | sort | flops 384 | bytes 1024 | tf_op jit(solution)/shard_map/jit(argsort)/sort | solution.py:25
  16.9 2.0 %sort.50 = (s32[64]{0:T(128)}, s32[64]{0:T(128)S(1)}) sort(s32[64]{0:T(128)S(1)} %get-tuple-element.9, s32[64]{0:T(128)S(1)} %iota.44), dimensions={0}, to_apply=%region_2.3 | sort | flops 384 | bytes 1024 | tf_op jit(solution)/shard_map/jit(argsort)/sort | solution.py:26
  19.0 0.1 iota_compare_fusion
  19.1 3.2 %and_select_fusion = bf16[64,128,128]{2,1,0:T(8,128)(2,1)S(1)} fusion(bf16[64,128,128]{2,1,0:T(8,128)(2,1)} %param.6, pred[64,128]{1,0:T(8,128)(4,1)S(1)} %get-tuple-element.14, pred[64,128]{1,0:T(8,128)(4,1)S(1)} %get-tuple-element.13), kind=kLoop, calls=%fused_computation.4 | loop fusion | flops 2097152 | bytes 4210688 | tf_op jit(solution)/shard_map/mul | solution.py:34
  22.3 2.1 %convolution_convert_fusion = bf16[8,8,128,128]{3,2,1,0:T(8,128)(2,1)} fusion(bf16[8,8,128,128]{3,2,1,0:T(8,128)(2,1)S(1)} %bitcast.27, bf16[1,8,128,128]{3,2,1,0:T(8,128)(2,1)S(1)} %copy-done.2), kind=kOutput, calls=%fused_computation.7 | convolution fusion | flops 269484032 | bytes 4456448 | tf_op jit(solution)/shard_map/ksab,snbc->ksnac/dot_general | solution.py:35
  24.5 36.5 %all-to-all-done = bf16[1,16,4,128,128]{4,3,2,0,1:T(8,128)(2,1)S(1)} async-done(((bf16[1,16,4,128,128]{4,3,2,0,1:T(8,128)(2,1)}), bf16[1,16,4,128,128]{4,3,2,0,1:T(8,128)(2,1)S(1)}, u32[]{:S(2)}, u32[]{:S(2)}) %all-to-all-start) | async-done | bytes 2097184 | tf_op jit(solution)/shard_map/all_to_all | solution.py:52
  61.0 2.2 %gather_fusion.2 = bf16[64,128,128]{2,1,0:T(8,128)(2,1)} fusion(bf16[64,128,128]{2,1,0:T(8,128)(2,1)S(1)} %bitcast.25, s32[1024]{0:T(1024)S(1)} %pad_clamp_fusion), kind=kCustom, calls=%fused_computation.2 | custom fusion | bytes 4194560 | tf_op jit(solution)/shard_map/gather | solution.py:53
  63.1 5.8 %fusion.6 = f32[64,128,128]{2,1,0:T(8,128)} fusion(bf16[64,128,128]{1,2,0:T(8,128)(2,1)} %bitcast.28, bf16[64,128,128]{2,1,0:T(8,128)(2,1)} %gather_fusion.2), kind=kOutput, calls=%fused_computation.38 | convolution fusion | flops 268435456 | bytes 8388608 | tf_op jit(solution)/shard_map/kjab,kjcb->jac/dot_general | solution.py:54
  68.9 16.2 %all-reduce.1 = bf16[64,128,128]{2,1,0:T(8,128)(2,1)S(1)} all-reduce(f32[64,128,128]{2,1,0:T(8,128)} %fusion.6), channel_id=1, replica_groups=mesh['sector'=16,'op'=2] {'op'}, use_global_device_ids=true, to_apply=%region_3.4 | all-reduce | flops 1048576 | bytes 6291456 | tf_op jit(solution)/shard_map/psum | solution.py:9
  85.1 1.5 %and_select_fusion.1 = bf16[64,64,128]{2,1,0:T(8,128)(2,1)} fusion(bf16[64,128,128]{2,1,0:T(8,128)(2,1)S(1)} %all-reduce.1, s32[]{:T(128)S(6)} %select_n.61, pred[64,128]{1,0:T(8,128)(4,1)S(1)} %get-tuple-element.14, pred[64,64]{1,0:T(8,128)(4,1)S(1)} %broadcast_compare_fusion), kind=kLoop, calls=%fused_computation.6 | loop fusion | flops 1048576 | bytes 2109444 | tf_op jit(solution)/shard_map/mul | solution.py:62
  (26 shorter events, 0.5 us)
Async XLA Ops:
  0.0 4.1 %copy-start = (bf16[1,8,128,128]{3,2,1,0:T(8,128)(2,1)S(1)}, bf16[1,8,128,128]{3,2,1,0:T(8,128)(2,1)}, u32[]{:S(2)}) copy-start(bf16[1,8,128,128]{3,2,1,0:T(8,128)(2,1)} %param.8) | copy-start | bytes 786436
  6.3 6.7 %copy-start.3 = (s32[128]{0:T(128)S(1)}, s32[128]{0:T(128)}, u32[]{:S(2)}) copy-start(s32[128]{0:T(128)} %param.9) | copy-start | bytes 1540
  6.3 7.8 %copy-start.1 = (s32[128]{0:T(128)S(1)}, s32[128]{0:T(128)}, u32[]{:S(2)}) copy-start(s32[128]{0:T(128)} %param.10) | copy-start | bytes 1540
  6.3 54.7 %all-to-all-start = ((bf16[1,16,4,128,128]{4,3,2,0,1:T(8,128)(2,1)}), bf16[1,16,4,128,128]{4,3,2,0,1:T(8,128)(2,1)S(1)}, u32[]{:S(2)}, u32[]{:S(2)}) async-start(bf16[1,16,4,128,128]{4,3,2,0,1:T(8,128)(2,1)} %bitcast.26), calls=%async_computation | async-start | bytes 4194304 | tf_op jit(solution)/shard_map/all_to_all | solution.py:52
  19.1 3.2 %copy-start.2 = (bf16[1,8,128,128]{3,2,1,0:T(8,128)(2,1)S(1)}, bf16[1,8,128,128]{3,2,1,0:T(8,128)(2,1)}, u32[]{:S(2)}) copy-start(bf16[1,8,128,128]{3,2,1,0:T(8,128)(2,1)} %param.7) | copy-start | bytes 786436
where the time goes:
time: 86.9 us; the launch traced here: 86.6 us
  waiting for transfers between devices  36.5 us (42%)
  blocking collectives  16.2 us (19%)
  other arithmetic  11.5 us (13%)
  matrix products  7.91 us (9%)
  local copies, waits for them, and re-layouts  7.65 us (9%)
  starting transfers between devices  6.74 us (8%)
    all_to_all x1, waiting for transfers between devices, per_device(): lax.all_to_all(outgoing, 'sector', split_axis=1, concat_axis=1, tiled=True)  36.5 us
    psum x1, blocking collectives, combine(): whole = lax.psum(partial_sum, 'op')  16.2 us
    all_to_all x1, starting transfers between devices, per_device(): lax.all_to_all(outgoing, 'sector', split_axis=1, concat_axis=1, tiled=True)  6.74 us
    dot_general x1, matrix products, per_device(): jnp.einsum('kjab,kjcb->jac', products, chosen, preferred_element_type=jnp...  5.76 us
    mul x1, other arithmetic, per_device(): masked = psi * keep_mask.astype(psi.dtype)  3.23 us
    gather x1, local copies, waits for them, and re-layouts, per_device(): right_env[:, arriving]  2.17 us
    gather x1, local copies, waits for them, and re-layouts, per_device(): received.reshape(term_count, blocks, block_width, block_width)[:, inverse]  2.16 us
    dot_general x1, matrix products, per_device(): jnp.einsum('ksab,snbc->ksnac', left_env, masked.reshape(sectors, coupled,...  2.15 us
  transfers between devices with their start and end apart: 1, of which 1 were waited for; matrix products, arithmetic and copies ran while one was open for 13% of the time, Pallas kernels for 0%

commit v1 on v0

--- a/solution.py
+++ b/solution.py
@@ -6,7 +6,7 @@
 
 def combine(partial_sum):
     row_count = partial_sum.shape[1] // lax.axis_size("op")
-    whole = lax.psum(partial_sum, "op")
+    whole = jnp.sum(lax.all_gather(partial_sum, "op"), axis=0)
     return lax.dynamic_slice_in_dim(whole, lax.axis_index("op") * row_count, row_count, 1)
 
 

time: 86.9 us -> 110 us (1.27)
  waiting for transfers between devices: 36.5 us -> 56.7 us
  blocking collectives: 16.2 us -> 0 us
  between operations: 0.11 us -> 13.5 us
  other arithmetic: 11.5 us -> 16.2 us
    all_gather x0 -> x1, waiting for transfers between devices: none -> 20.2 us  [combine(): whole = jnp.sum(lax.all_gather(partial_sum, 'op'), axis=0)]
    psum x1 -> x0, blocking collectives: 16.2 us -> none  [combine(): whole = lax.psum(partial_sum, 'op')]
    reduce_sum x0 -> x1, other arithmetic: none -> 4.64 us  [combine(): whole = jnp.sum(lax.all_gather(partial_sum, 'op'), axis=0)]
  transfers between devices with their start and end apart: 1 -> 2, of which waited for: 1 -> 2; matrix products, arithmetic and copies ran while one was open for 13% -> 11% of each run, Pallas kernels for 0% -> 0%
where the time goes in v1:
time: 110 us; the launch traced here: 109 us
  waiting for transfers between devices  56.7 us (52%)
  other arithmetic  16.2 us (15%)
  between operations  13.5 us (12%)
  matrix products  7.98 us (7%)
  local copies, waits for them, and re-layouts  7.55 us (7%)
  starting transfers between devices  6.78 us (6%)
    all_to_all x1, waiting for transfers between devices, per_device(): lax.all_to_all(outgoing, 'sector', split_axis=1, concat_axis=1, tiled=True)  36.5 us
    all_gather x1, waiting for transfers between devices, combine(): whole = jnp.sum(lax.all_gather(partial_sum, 'op'), axis=0)  20.2 us
    all_to_all x1, starting transfers between devices, per_device(): lax.all_to_all(outgoing, 'sector', split_axis=1, concat_axis=1, tiled=True)  6.74 us
    dot_general x1, matrix products, per_device(): jnp.einsum('kjab,kjcb->jac', products, chosen, preferred_element_type=jnp...  5.81 us
    reduce_sum x1, other arithmetic, combine(): whole = jnp.sum(lax.all_gather(partial_sum, 'op'), axis=0)  4.64 us
    mul x1, other arithmetic, per_device(): masked = psi * keep_mask.astype(psi.dtype)  3.23 us
  transfers between devices with their start and end apart: 2, of which 2 were waited for; matrix products, arithmetic and copies ran while one was open for 11% of the time, Pallas kernels for 0%

profile of v1, /device:TPU:13, one launch (start us, length us, event | category | flops | bytes accessed | tf_op | source)
XLA Modules:
  0.0 108.7 jit_solution(3984864027287928750)
XLA Ops:
  6.5 0.8 reshape.167
  7.3 0.7 fusion.4
  8.1 0.1 copy.23
  8.2 1.0 sort.48
  9.2 0.1 copy.24
  9.3 0.1 reshape.200
  9.4 0.8 gather_fusion.3
  10.4 0.1 copy.26
  10.5 0.1 sub.31
  10.6 2.1 %gather_fusion.1 = bf16[64,128,128]{2,1,0:T(8,128)(2,1)} fusion(bf16[8,128,128]{2,1,0:T(8,128)(2,1)S(1)} %bitcast.25, s32[1024]{0:T(1024)S(1)} %pad_clamp_fusion.1), kind=kCustom, calls=%fused_computation.1 | custom fusion | bytes 4194560 | tf_op jit(solution)/shard_map/gather | solution.py:49
  12.7 6.7 %all-to-all-start = ((bf16[1,16,4,128,128]{4,3,2,0,1:T(8,128)(2,1)}), bf16[1,16,4,128,128]{4,3,2,0,1:T(8,128)(2,1)S(1)}, u32[]{:S(2)}, u32[]{:S(2)}) async-start(bf16[1,16,4,128,128]{4,3,2,0,1:T(8,128)(2,1)} %bitcast.28), calls=%async_computation | async-start | bytes 4194304 | tf_op jit(solution)/shard_map/all_to_all | solution.py:52
  19.8 0.8 iota_add_fusion.1
  20.6 0.8 gather_fusion
  21.3 2.0 %sort.49 = (s32[64]{0:T(128)}, s32[64]{0:T(128)S(1)}) sort(s32[64]{0:T(128)S(1)} %get-tuple-element.11, s32[64]{0:T(128)S(1)} %iota.43), dimensions={0}, to_apply=%region_1.2 | sort | flops 384 | bytes 1024 | tf_op jit(solution)/shard_map/jit(argsort)/sort | solution.py:25
  23.4 2.0 %sort.50 = (s32[64]{0:T(128)}, s32[64]{0:T(128)S(1)}) sort(s32[64]{0:T(128)S(1)} %get-tuple-element.9, s32[64]{0:T(128)S(1)} %iota.44), dimensions={0}, to_apply=%region_2.3 | sort | flops 384 | bytes 1024 | tf_op jit(solution)/shard_map/jit(argsort)/sort | solution.py:26
  25.4 0.1 iota_compare_fusion
  25.5 3.2 %and_select_fusion = bf16[64,128,128]{2,1,0:T(8,128)(2,1)S(1)} fusion(bf16[64,128,128]{2,1,0:T(8,128)(2,1)} %param.6, pred[64,128]{1,0:T(8,128)(4,1)S(1)} %get-tuple-element.14, pred[64,128]{1,0:T(8,128)(4,1)S(1)} %get-tuple-element.13), kind=kLoop, calls=%fused_computation.4 | loop fusion | flops 2097152 | bytes 4210688 | tf_op jit(solution)/shard_map/mul | solution.py:34
  28.8 2.2 %convolution_convert_fusion = bf16[8,8,128,128]{3,2,1,0:T(8,128)(2,1)} fusion(bf16[8,8,128,128]{3,2,1,0:T(8,128)(2,1)S(1)} %bitcast.29, bf16[1,8,128,128]{3,2,1,0:T(8,128)(2,1)S(1)} %copy-done.2), kind=kOutput, calls=%fused_computation.7 | convolution fusion | flops 269484032 | bytes 4456448 | tf_op jit(solution)/shard_map/ksab,snbc->ksnac/dot_general | solution.py:35
  31.0 36.5 %all-to-all-done = bf16[1,16,4,128,128]{4,3,2,0,1:T(8,128)(2,1)S(1)} async-done(((bf16[1,16,4,128,128]{4,3,2,0,1:T(8,128)(2,1)}), bf16[1,16,4,128,128]{4,3,2,0,1:T(8,128)(2,1)S(1)}, u32[]{:S(2)}, u32[]{:S(2)}) %all-to-all-start) | async-done | bytes 2097184 | tf_op jit(solution)/shard_map/all_to_all | solution.py:52
  67.5 2.1 %gather_fusion.2 = bf16[64,128,128]{2,1,0:T(8,128)(2,1)} fusion(bf16[64,128,128]{2,1,0:T(8,128)(2,1)S(1)} %bitcast.27, s32[1024]{0:T(1024)S(1)} %pad_clamp_fusion), kind=kCustom, calls=%fused_computation.2 | custom fusion | bytes 4194560 | tf_op jit(solution)/shard_map/gather | solution.py:53
  69.6 5.8 %fusion.6 = f32[64,128,128]{2,1,0:T(8,128)} fusion(bf16[64,128,128]{1,2,0:T(8,128)(2,1)} %bitcast.30, bf16[64,128,128]{2,1,0:T(8,128)(2,1)} %gather_fusion.2), kind=kOutput, calls=%fused_computation.38 | convolution fusion | flops 268435456 | bytes 8388608 | tf_op jit(solution)/shard_map/kjab,kjcb->jac/dot_general | solution.py:54
  75.5 20.2 %all-gather.3.cloned.1.call-done = f32[128,128,128]{2,1,0:T(8,128)} async-done(((f32[64,128,128]{2,1,0:T(8,128)}), f32[128,128,128]{2,1,0:T(8,128)}) %all-gather.3.cloned.1.call-update) | async-done | bytes 8388624 | tf_op jit(solution)/shard_map/all_gather | solution.py:9
  95.7 4.6 %reduce_sum.9 = bf16[64,128,128]{2,1,0:T(8,128)(2,1)S(1)} reduce(f32[2,64,128,128]{3,2,1,0:T(8,128)} %bitcast.26, f32[]{:T(128)} %constant.65.clone.1), dimensions={0}, to_apply=%region_3.4 | reduce | flops 1048576 | bytes 10485764 | tf_op jit(solution)/shard_map/reduce_sum | solution.py:9
  100.4 1.5 %and_select_fusion.1 = bf16[64,64,128]{2,1,0:T(8,128)(2,1)} fusion(bf16[64,128,128]{2,1,0:T(8,128)(2,1)S(1)} %reduce_sum.9, s32[]{:T(128)S(6)} %select_n.61, pred[64,128]{1,0:T(8,128)(4,1)S(1)} %get-tuple-element.14, pred[64,64]{1,0:T(8,128)(4,1)S(1)} %broadcast_compare_fusion), kind=kLoop, calls=%fused_computation.6 | loop fusion | flops 1048576 | bytes 2109444 | tf_op jit(solution)/shard_map/mul | solution.py:62
  (29 shorter events, 0.7 us)
Async XLA Ops:
  6.5 4.1 %copy-start = (bf16[1,8,128,128]{3,2,1,0:T(8,128)(2,1)S(1)}, bf16[1,8,128,128]{3,2,1,0:T(8,128)(2,1)}, u32[]{:S(2)}) copy-start(bf16[1,8,128,128]{3,2,1,0:T(8,128)(2,1)} %param.8) | copy-start | bytes 786436
  12.7 6.8 %copy-start.3 = (s32[128]{0:T(128)S(1)}, s32[128]{0:T(128)}, u32[]{:S(2)}) copy-start(s32[128]{0:T(128)} %param.9) | copy-start | bytes 1540
  12.7 7.8 %copy-start.1 = (s32[128]{0:T(128)S(1)}, s32[128]{0:T(128)}, u32[]{:S(2)}) copy-start(s32[128]{0:T(128)} %param.10) | copy-start | bytes 1540
  12.7 54.7 %all-to-all-start = ((bf16[1,16,4,128,128]{4,3,2,0,1:T(8,128)(2,1)}), bf16[1,16,4,128,128]{4,3,2,0,1:T(8,128)(2,1)S(1)}, u32[]{:S(2)}, u32[]{:S(2)}) async-start(bf16[1,16,4,128,128]{4,3,2,0,1:T(8,128)(2,1)} %bitcast.28), calls=%async_computation | async-start | bytes 4194304 | tf_op jit(solution)/shard_map/all_to_all | solution.py:52
  19.5 76.2 %all-gather.3.cloned.1.call-start = ((), (), s32[]{:S(2)}) async-start(), calls=%async_computation.1 | async-start | bytes 12582912 | tf_op jit(solution)/shard_map/all_gather | solution.py:9
  25.5 3.2 %copy-start.2 = (bf16[1,8,128,128]{3,2,1,0:T(8,128)(2,1)S(1)}, bf16[1,8,128,128]{3,2,1,0:T(8,128)(2,1)}, u32[]{:S(2)}) copy-start(bf16[1,8,128,128]{3,2,1,0:T(8,128)(2,1)} %param.7) | copy-start | bytes 786436
Sparse Core Ops, SparseCore 0:
  75.5 20.1 all-gather.2
